TPU v7x, 32 devices: a whole 2x2x4 slice. The times are simulated.
32 devices in a mesh: layer: 4 (over y, core), feat: 8 (over z, x).
Axes of the slice: x: 2, y: 2, z: 4, core: 2. Of those that a mesh axis runs over, the one named last changes fastest.
Arguments:
- acts: bfloat16 [4, 768, 1024], P('layer'), may hold values from -6 to 6
- targets: bfloat16 [4, 768, 1024], P('layer', 'feat'), may hold values from -6 to 6
- enc_weight: bfloat16 [4, 1024, 20480], P('layer', None, 'feat'), may hold values from -0.1875 to 0.1875
- enc_bias: float32 [4, 20480], P('layer', 'feat'), may hold values from -3 to 3
- dec_weight: bfloat16 [4, 20480, 2, 1024], P('layer', 'feat'), may hold values from -0.0390625 to 0.0390625
- dec_bias: float32 [4, 1024], P('layer'), may hold values from -3 to 3
Outputs:
- errors: float32 [4, 768, 1024], P('layer', 'feat')
- enc_grad: bfloat16 [4, 1024, 20480], P('layer', None, 'feat')
All inputs are finite; a program needn't handle non-finite values.
Results may differ from a plain program's by a relative error of at most 0.006.
Values may be sent and summed in bfloat16 or wider, within the bound.
A program may use at most 128 MiB of HBM per device.

v0:
```python
import functools

import jax
import jax.numpy as jnp
from jax import lax
from jax.experimental import pallas as pl
from jax.experimental.pallas import tpu as pltpu
from jax.sharding import PartitionSpec as P

MESH = pl.DeviceIdType.MESH
CHUNKS = 4


def inner_of(n):
    return max(d for d in range(1, n + 1) if n % d == 0 and d * d <= n)


def exchange_kernel(
    layers, m, o, latent_ref, dec_ref, targets_ref, bias_ref, acts_ref,
    errors_ref, gath_ref, foll_ref, turned_ref,
    dec, later, arrived, sums, near, mids, far, mine,
    dec_sem, up_send, up_recv, near_send, near_recv, far_send, far_recv,
    out_send, out_recv, in_send, in_recv, down_send, down_recv,
):
    layer = lax.axis_index("layer")
    me = lax.axis_index("feat")
    z, x = me // m, lax.rem(me, m)
    above = lax.rem(layer + 1, layers)
    below = lax.rem(layer + layers - 1, layers)
    tokens, width = gath_ref.shape
    rows = tokens // (m * o)
    wide = width // CHUNKS

    def at(dz, dx):
        return lax.rem(z + dz + o, o) * m + lax.rem(x + dx + m, m)

    def rows_of(i):
        return pl.ds(pl.multiple_of(i * rows, rows), rows)

    def cols(c):
        return pl.ds(pl.multiple_of(c * wide, wide), wide)

    def load(w, c):
        return pltpu.make_async_copy(
            dec_ref.at[w, :, cols(c)], dec.at[w, :, cols(c)], dec_sem.at[w, c]
        )

    def remote(src, dst, send, recv, where):
        return pltpu.make_async_remote_copy(
            src_ref=src, dst_ref=dst, send_sem=send, recv_sem=recv,
            device_id=where, device_id_type=MESH,
        )

    def up(c):
        return remote(later.at[:, cols(c)], arrived.at[:, cols(c)], up_send.at[c], up_recv.at[c], (above, me))

    def add_near(c, q, r):
        j = (q - 1) * o + r
        return remote(
            sums.at[rows_of(at(r, q)), cols(c)], near.at[j, :, cols(c)],
            near_send.at[c, j], near_recv.at[c, j], (layer, at(0, q)),
        )

    def add_far(c, r):
        return remote(
            mids.at[r - 1, :, cols(c)], far.at[r - 1, :, cols(c)],
            far_send.at[c, r - 1], far_recv.at[c, r - 1], (layer, at(r, 0)),
        )

    def give_far(c, r, owner):
        spot = gath_ref.at[rows_of(owner), cols(c)]
        return remote(spot, spot, out_send.at[c, r - 1], out_recv.at[c, r - 1], (layer, at(r, 0)))

    def give_near(c, q, r, owner):
        j = (q - 1) * o + r
        spot = gath_ref.at[rows_of(owner), cols(c)]
        return remote(spot, spot, in_send.at[c, j], in_recv.at[c, j], (layer, at(0, q)))

    def down(c, q, r):
        owner = at(-r, -q)
        j = q * o + r
        return remote(
            gath_ref.at[rows_of(owner), cols(c)], foll_ref.at[rows_of(owner), cols(c)],
            down_send.at[c, j], down_recv.at[c, j], (below, me),
        )

    for w in (1, 0):
        for c in range(CHUNKS):
            load(w, c).start()

    barrier = pltpu.get_barrier_semaphore()
    for to in (
        [(layer, at(0, q)) for q in range(1, m)]
        + [(layer, at(r, 0)) for r in range(1, o)]
        + [(above, me), (below, me)]
    ):
        pl.semaphore_signal(barrier, inc=1, device_id=to, device_id_type=MESH)
    pl.semaphore_wait(barrier, m + o)

    @pl.loop(0, CHUNKS)
    def _(c):
        load(1, c).wait()
        later[:, cols(c)] = jnp.dot(
            latent_ref[...], dec[1, :, cols(c)], preferred_element_type=jnp.float32
        ).astype(jnp.bfloat16)
        up(c).start()

    @pl.loop(0, CHUNKS)
    def _(c):
        load(0, c).wait()
        own = jnp.dot(latent_ref[...], dec[0, :, cols(c)], preferred_element_type=jnp.float32)
        up(c).wait_recv()
        carried = jnp.where(layer > 0, arrived[:, cols(c)].astype(jnp.float32), 0.0)
        sums[:, cols(c)] = (own + carried).astype(jnp.bfloat16)
        for q in range(1, m):
            for r in range(o):
                add_near(c, q, r).start()

    turned_ref[...] = acts_ref[...].T

    @pl.loop(0, CHUNKS)
    def _(c):
        for r in (*range(1, o), 0):
            total = sums[rows_of(at(r, 0)), cols(c)].astype(jnp.float32)
            for q in range(1, m):
                add_near(c, q, r).wait_recv()
                total = total + near[(q - 1) * o + r, :, cols(c)].astype(jnp.float32)
            if r:
                mids[r - 1, :, cols(c)] = total.astype(jnp.bfloat16)
                add_far(c, r).start()
            else:
                mine[:, cols(c)] = total

    @pl.loop(0, CHUNKS)
    def _(c):
        total = mine[:, cols(c)]
        for r in range(1, o):
            add_far(c, r).wait_recv()
            total = total + far[r - 1, :, cols(c)].astype(jnp.float32)
        errors = total + bias_ref[:, cols(c)] - targets_ref[:, cols(c)].astype(jnp.float32)
        errors_ref[:, cols(c)] = errors
        gath_ref[rows_of(me), cols(c)] = errors.astype(jnp.bfloat16)
        for r in range(1, o):
            give_far(c, r, me).start()
        for q in range(1, m):
            give_near(c, q, 0, me).start()
        down(c, 0, 0).start()

    @pl.loop(0, CHUNKS)
    def _(c):
        for r in range(1, o):
            owner = at(-r, 0)
            give_far(c, r, owner).wait_recv()
            for q in range(1, m):
                give_near(c, q, r, owner).start()
            down(c, 0, r).start()

    @pl.loop(0, CHUNKS)
    def _(c):
        for q in range(1, m):
            for r in range(o):
                give_near(c, q, r, at(-r, -q)).wait_recv()
                down(c, q, r).start()

    @pl.loop(0, CHUNKS)
    def _(c):
        up(c).wait_send()
        for r in range(1, o):
            add_far(c, r).wait_send()
            give_far(c, r, me).wait_send()
        for r in range(o):
            for q in range(1, m):
                add_near(c, q, r).wait_send()
                give_near(c, q, r, at(-r, 0)).wait_send()
            for q in range(m):
                down(c, q, r).wait_recv()
                down(c, q, r).wait_send()

    @pl.when(layer == layers - 1)
    def _():
        foll_ref[...] = jnp.zeros_like(foll_ref)


def exchange(layers, n, latent, dec, targets, bias, acts):
    tokens, features = latent.shape
    width = dec.shape[2]
    rows = tokens // n
    m = inner_of(n)
    o = n // m
    half = jnp.bfloat16
    vmem = pl.BlockSpec(memory_space=pltpu.VMEM)
    dma = pltpu.SemaphoreType.DMA
    pairs = [(CHUNKS, k) for k in ((m - 1) * o, o - 1, o - 1, (m - 1) * o, n)]
    return pl.pallas_call(
        functools.partial(exchange_kernel, layers, m, o),
        out_shape=(
            jax.ShapeDtypeStruct((rows, width), jnp.float32),
            jax.ShapeDtypeStruct((tokens, width), half),
            jax.ShapeDtypeStruct((tokens, width), half),
            jax.ShapeDtypeStruct((width, tokens), half),
        ),
        in_specs=[vmem, pl.BlockSpec(memory_space=pl.ANY), vmem, vmem, vmem],
        out_specs=(vmem, vmem, vmem, vmem),
        scratch_shapes=[
            pltpu.VMEM((2, features, width), half),
            pltpu.VMEM((tokens, width), half),
            pltpu.VMEM((tokens, width), half),
            pltpu.VMEM((tokens, width), half),
            pltpu.VMEM(((m - 1) * o, rows, width), half),
            pltpu.VMEM((o - 1, rows, width), half),
            pltpu.VMEM((o - 1, rows, width), half),
            pltpu.VMEM((rows, width), jnp.float32),
            dma((2, CHUNKS)),
            dma((CHUNKS,)),
            dma((CHUNKS,)),
            *[dma(p) for p in pairs for _ in range(2)],
        ],
        compiler_params=pltpu.CompilerParams(
            collective_id=0, has_side_effects=True, vmem_limit_bytes=48 * 2**20
        ),
        name="exchange",
    )(latent, dec, targets, bias, acts)


def grad_kernel(scale, gath_ref, foll_ref, turned_ref, dec_ref, pre_ref, out_ref):
    grad_latent = contract_width(gath_ref[...], dec_ref[0]) + contract_width(foll_ref[...], dec_ref[1])
    deriv = jax.nn.sigmoid(4.0 * pre_ref[...])
    grad_pre = (grad_latent * deriv).astype(jnp.bfloat16)
    total = jnp.dot(turned_ref[...], grad_pre, preferred_element_type=jnp.float32)
    out_ref[...] = (total * scale).astype(jnp.bfloat16)


def encoder_grad(gathered, following, turned, dec, pre):
    tokens, features = pre.shape
    width = turned.shape[0]
    tile = 256
    vmem = pl.BlockSpec(memory_space=pltpu.VMEM)
    return pl.pallas_call(
        functools.partial(grad_kernel, tokens ** (-0.5)),
        grid=(features // tile,),
        out_shape=jax.ShapeDtypeStruct((width, features), jnp.bfloat16),
        in_specs=[
            vmem, vmem, vmem,
            pl.BlockSpec((2, tile, width), lambda i: (0, i, 0)),
            pl.BlockSpec((tokens, tile), lambda i: (0, i)),
        ],
        out_specs=pl.BlockSpec((width, tile), lambda i: (0, i)),
        compiler_params=pltpu.CompilerParams(vmem_limit_bytes=40 * 2**20),
        name="encoder_grad",
    )(gathered, following, turned, dec, pre)


def contract_width(errs, decoder):
    return lax.dot_general(
        errs, decoder, (((1,), (1,)), ((), ())), preferred_element_type=jnp.float32
    )


def local(layers, n, acts, targets, enc_weight, enc_bias, dec_weight, dec_bias):
    inputs = acts[0]
    weight = enc_weight[0]
    bias = enc_bias[0]
    dec = jnp.transpose(dec_weight[0], (1, 0, 2))
    pre = jnp.dot(inputs, weight, preferred_element_type=jnp.float32) + bias
    latent = (jax.nn.softplus(4.0 * pre) * 0.25).astype(jnp.bfloat16)
    errors, gathered, following, turned = exchange(
        layers, n, latent, dec, targets[0], dec_bias, inputs
    )
    enc_grad = encoder_grad(gathered, following, turned, dec, pre)
    return (errors[None], enc_grad[None])


def solution(mesh):
    return jax.shard_map(
        functools.partial(local, mesh.shape["layer"], mesh.shape["feat"]),
        mesh=mesh,
        in_specs=(
            P("layer", None, None),
            P("layer", "feat", None),
            P("layer", None, "feat"),
            P("layer", "feat"),
            P("layer", "feat", None, None),
            P("layer", None),
        ),
        out_specs=(P("layer", "feat", None), P("layer", None, "feat")),
        check_vma=False,
    )
```

profile of v0, /device:TPU:1, one launch (start us, length us, event | category | flops | bytes accessed | tf_op | source)
XLA Modules:
  0.0 126.6 jit_solution(4763825324734237872)
XLA Ops:
  0.6 0.7 reduce
  1.4 15.9 %fusion.1 = (bf16[768,2560]{1,0:T(8,128)(2,1)}, f32[768,2560]{1,0:T(8,128)}) fusion(f32[2560]{0:T(1024)S(1)} %reduce, bf16[1,1024,2560]{2,1,0:T(8,128)(2,1)} %param.8, bf16[1,768,1024]{2,1,0:T(8,128)(2,1)} %param.6), kind=kOutput, calls=%fused_computation.3 | convolution fusion | flops 4046192640 | bytes 18622464 | tf_op jit(solution)/shard_map/dot_general | solution.py:264
  17.2 0.0 copy-start.1
  17.2 0.0 copy-start.2
  17.3 11.3 %copy.10 = bf16[1,2560,2,1024]{3,1,2,0:T(8,128)(2,1)} copy(bf16[1,2560,2,1024]{3,2,1,0:T(2,128)(2,1)} %param.10) | data formatting | bytes 20971520 | tf_op args[4]
  28.6 0.0 copy-done.1
  28.6 0.0 copy-done.2
  28.6 0.0 copy-start
  28.6 72.7 %exchange.1 = (f32[96,1024]{1,0:T(8,128)S(1)}, bf16[768,1024]{1,0:T(8,128)(2,1)S(1)}, bf16[768,1024]{1,0:T(8,128)(2,1)S(1)}, bf16[1024,768]{1,0:T(8,128)(2,1)S(1)}) custom-call(bf16[768,2560]{1,0:T(8,128)(2,1)} %get-tuple-element.10.latent_ref, bf16[2,2560,1024]{2,1,0:T(8,128)(2,1)} %bitcast.20, bf16[96,1024]{1,0:T(8,128)(2,1)S(1)} %bitcast.19, ...), custom_call_target="tpu_custom_call" | custom-call | tf_op jit(solution)/shard_map/exchange/pallas_call | solution.py:194
  101.3 0.0 copy-done
  101.3 24.6 %encoder_grad.1 = bf16[1024,2560]{1,0:T(8,128)(2,1)} custom-call(bf16[768,1024]{1,0:T(8,128)(2,1)S(1)} %get-tuple-element.7.gath_ref, bf16[768,1024]{1,0:T(8,128)(2,1)S(1)} %get-tuple-element.8.foll_ref, bf16[1024,768]{1,0:T(8,128)(2,1)S(1)} %get-tuple-element.9.turned_ref, bf16[2,2560,1024]{2,1,0:T(8,128)(2,1)} %bitcast.21, f32[768,2560]{1,0:T(8,128)S(1)} %copy-done), custom_call_target="tpu_custom_call" | custom-call | tf_op jit(solution)/shard_map/encoder_grad/pallas_call | solution.py:238
  125.9 0.7 copy.12
Async XLA Ops:
  17.2 11.3 %copy-start.1 = (bf16[1,96,1024]{2,1,0:T(8,128)(2,1)S(1)}, bf16[1,96,1024]{2,1,0:T(8,128)(2,1)}, u32[]{:S(2)}) copy-start(bf16[1,96,1024]{2,1,0:T(8,128)(2,1)} %param.7) | copy-start | bytes 589828
  17.2 11.3 %copy-start.2 = (f32[1,1024]{1,0:T(1,128)S(1)}, f32[1,1024]{1,0:T(1,128)}, u32[]{:S(2)}) copy-start(f32[1,1024]{1,0:T(1,128)} %bias_ref.1) | copy-start | bytes 12292
  28.6 72.7 %copy-start = (f32[768,2560]{1,0:T(8,128)S(1)}, f32[768,2560]{1,0:T(8,128)}, u32[]{:S(2)}) copy-start(f32[768,2560]{1,0:T(8,128)} %get-tuple-element.11.pre_ref) | copy-start | bytes 23592964
where the time goes:
time: 127 us
  Pallas kernels  97.3 us (77%)
  matrix products  15.9 us (13%)
  local copies, waits for them, and re-layouts  12.1 us (10%)
    pallas_call x1, Pallas kernels, exchange(): pl.pallas_call(functools.partial(exchange_kernel, layers, m, o), out_shap...  72.7 us
    pallas_call x1, Pallas kernels, encoder_grad(): pl.pallas_call(functools.partial(grad_kernel, tokens ** (-0.5)), grid=(fe...  24.6 us
    dot_general x1, matrix products, local(): pre = jnp.dot(inputs, weight, preferred_element_type=jnp.float32) + bias  15.9 us
    unnamed x8, local copies, waits for them, and re-layouts  12.1 us

commit v1 on v0

v1 whole, which is shorter than its diff:
```python
import functools

import jax
import jax.numpy as jnp
from jax import lax
from jax.experimental import pallas as pl
from jax.experimental.pallas import tpu as pltpu
from jax.sharding import PartitionSpec as P

MESH = pl.DeviceIdType.MESH
PIECES = 2


def inner_of(n):
    return max(d for d in range(1, n + 1) if n % d == 0 and d * d <= n)


def chunks_of(rows):
    return next((c for c in (3, 2) if rows % (16 * c) == 0), 1)


def tile_of(features):
    return features // 2 if features % 256 == 0 else features


def contract_width(errs, decoder):
    return lax.dot_general(
        errs, decoder, (((1,), (1,)), ((), ())), preferred_element_type=jnp.float32
    )


def step_kernel(
    layers, m, o, acts_hbm, enc_hbm, dec_hbm, enc_bias_ref, targets_ref, bias_ref,
    errors_ref, grad_ref, acts,
    enc, raw, dec, deriv, latent, own, later, arrived, sums, near, mids, far, gath, foll,
    acts_sem, enc_sem, dec_sem, up_send, up_recv, near_send, near_recv, far_send, far_recv,
    out_send, out_recv, in_send, in_recv, down_send, down_recv,
):
    layer = lax.axis_index("layer")
    me = lax.axis_index("feat")
    z, x = me // m, lax.rem(me, m)
    above = lax.rem(layer + 1, layers)
    below = lax.rem(layer + layers - 1, layers)
    chunks, block, width = later.shape
    rows = block // (m * o)
    features = enc.shape[1]
    tile = tile_of(features)
    tiles = features // tile
    raws = raw.shape[0] // dec_sem.shape[0]
    wide = width // PIECES

    def at(zz, xx):
        return lax.rem(zz, o) * m + lax.rem(xx, m)

    def cols(h):
        return pl.ds(pl.multiple_of(h * wide, wide), wide)

    def feats(t):
        return pl.ds(pl.multiple_of(t * tile, tile), tile)

    def remote(src, dst, send, recv, where):
        return pltpu.make_async_remote_copy(
            src_ref=src, dst_ref=dst, send_sem=send, recv_sem=recv,
            device_id=where, device_id_type=MESH,
        )

    def load_acts(c, q):
        return pltpu.make_async_copy(acts_hbm.at[:, q, c], acts.at[c, q], acts_sem.at[c, q])

    def load_enc(t):
        return pltpu.make_async_copy(enc_hbm.at[:, feats(t)], enc.at[:, feats(t)], enc_sem.at[t])

    def load_dec(i):
        part = pl.ds(pl.multiple_of(i * raws, raws), raws)
        return pltpu.make_async_copy(dec_hbm.at[part], raw.at[part], dec_sem.at[i])

    def up(c, h):
        return remote(
            later.at[c, :, cols(h)], arrived.at[c, :, cols(h)],
            up_send.at[c, h], up_recv.at[c, h], (above, me),
        )

    def add_near(c, h, q):
        to = lax.rem(x + q, m)
        return remote(
            sums.at[c, to, :, :, cols(h)], near.at[c, q - 1, :, :, cols(h)],
            near_send.at[c, h, q - 1], near_recv.at[c, h, q - 1], (layer, at(z, to)),
        )

    def add_far(c, h, r):
        to = lax.rem(z + r, o)
        return remote(
            mids.at[c, to, :, cols(h)], far.at[c, r - 1, :, cols(h)],
            far_send.at[c, h, r - 1], far_recv.at[c, h, r - 1], (layer, at(to, x)),
        )

    def give_far(c, h, r, owner):
        spot = gath.at[c, x, owner, :, cols(h)]
        return remote(spot, spot, out_send.at[c, h, r - 1], out_recv.at[c, h, r - 1], (layer, at(z + r, x)))

    def give_near(c, h, q, column):
        spot = gath.at[c, column, :, :, cols(h)]
        return remote(spot, spot, in_send.at[c, h, q - 1], in_recv.at[c, h, q - 1], (layer, at(z, x + q)))

    def down(c, h, q):
        column = lax.rem(x + m - q, m)
        return remote(
            gath.at[c, column, :, :, cols(h)], foll.at[c, column, :, :, cols(h)],
            down_send.at[c, h, q], down_recv.at[c, h, q], (below, me),
        )

    def encode(c, t):
        lhs = acts[c].reshape(block, width)
        pre = jnp.dot(lhs, enc[:, feats(t)], preferred_element_type=jnp.float32)
        scaled = 4.0 * (pre + enc_bias_ref[:, feats(t)])
        shrunk = jnp.exp(-jnp.abs(scaled))
        latent[:, feats(t)] = ((jnp.maximum(scaled, 0.0) + jnp.log1p(shrunk)) * 0.25).astype(jnp.bfloat16)
        part = 1.0 / (1.0 + shrunk)
        deriv[c, :, feats(t)] = jnp.where(scaled >= 0.0, part, shrunk * part)

    def decode_later(c, h):
        later[c, :, cols(h)] = jnp.dot(
            latent[...], dec[1, :, cols(h)], preferred_element_type=jnp.float32
        ).astype(jnp.bfloat16)

        @pl.when(layer < layers - 1)
        def _():
            up(c, h).start()

    def decode_own(c, h):
        own[lax.rem(c, 2), :, cols(h)] = jnp.dot(latent[...], dec[0, :, cols(h)], preferred_element_type=jnp.float32)

    def send_near(c, h):
        @pl.when(layer > 0)
        def _():
            up(c, h).wait_recv()

        carried = jnp.where(layer > 0, arrived[c, :, cols(h)].astype(jnp.float32), 0.0)
        total = (own[lax.rem(c, 2), :, cols(h)] + carried).astype(jnp.bfloat16)
        sums[c, :, :, :, cols(h)] = total.reshape(m, o, rows, wide)
        for q in range(1, m):
            add_near(c, h, q).start()

    def send_far(c, h):
        total = sums[c, x, :, :, cols(h)].astype(jnp.float32)
        for q in range(1, m):
            add_near(c, h, q).wait_recv()
            total = total + near[c, q - 1, :, :, cols(h)].astype(jnp.float32)
        mids[c, :, :, cols(h)] = total.astype(jnp.bfloat16)
        for r in range(1, o):
            add_far(c, h, r).start()

    def give(c, h):
        total = sums[c, x, z, :, cols(h)].astype(jnp.float32)
        for q in range(1, m):
            total = total + near[c, q - 1, z, :, cols(h)].astype(jnp.float32)
        for r in range(1, o):
            add_far(c, h, r).wait_recv()
            total = total + far[c, r - 1, :, cols(h)].astype(jnp.float32)
        errors = total + bias_ref[:, cols(h)] - targets_ref[c, :, cols(h)].astype(jnp.float32)
        errors_ref[c, :, cols(h)] = errors
        gath[c, x, z, :, cols(h)] = errors.astype(jnp.bfloat16)
        for r in range(1, o):
            give_far(c, h, r, z).start()

    def pass_near(c, h):
        for r in range(1, o):
            give_far(c, h, r, lax.rem(z + o - r, o)).wait_recv()
        for q in range(1, m):
            give_near(c, h, q, x).start()

        @pl.when(layer > 0)
        def _():
            down(c, h, 0).start()

    def pass_down(c, h):
        for q in range(1, m):
            give_near(c, h, q, lax.rem(x + m - q, m)).wait_recv()

            @pl.when(layer > 0)
            def _():
                down(c, h, q).start()

    def gradient(c):
        @pl.when(layer < layers - 1)
        def _():
            for h in range(PIECES):
                for q in range(m):
                    down(c, h, q).wait_recv()

        @pl.loop(0, tiles)
        def _(t):
            grad = contract_width(gath[c].reshape(block, width), dec[0, feats(t), :])
            grad = grad + contract_width(foll[c].reshape(block, width), dec[1, feats(t), :])
            grad_ref[c, :, feats(t)] = (grad * deriv[c, :, feats(t)]).astype(jnp.bfloat16)

    for q in range(m):
        load_acts(0, q).start()
    for t in range(tiles):
        load_enc(t).start()
    for i in range(dec_sem.shape[0]):
        load_dec(i).start()
    for c in range(1, chunks):
        for q in range(m):
            load_acts(c, q).start()

    @pl.when(layer == layers - 1)
    def _():
        foll[...] = jnp.zeros_like(foll)

    barrier = pltpu.get_barrier_semaphore()
    for to in (
        [(layer, at(z, x + q)) for q in range(1, m)]
        + [(layer, at(z + r, x)) for r in range(1, o)]
        + [(above, me), (below, me)]
    ):
        pl.semaphore_signal(barrier, inc=1, device_id=to, device_id_type=MESH)

    for q in range(m):
        load_acts(0, q).wait()

    @pl.loop(0, tiles)
    def _(t):
        load_enc(t).wait()
        encode(0, t)

    @pl.loop(0, dec_sem.shape[0])
    def _(i):
        load_dec(i).wait()
        part = pl.ds(pl.multiple_of(i * raws, raws), raws)
        dec[:, part, :] = jnp.transpose(raw[part], (1, 0, 2))

    for c in range(1, chunks):
        for q in range(m):
            load_acts(c, q).wait()

    pl.semaphore_wait(barrier, m + o)

    @pl.loop(0, chunks)
    def _(c):
        def earlier(back, action, h):
            @pl.when(c >= back)
            def _():
                action(c - back, h)

        decode_later(c, 0)
        earlier(1, send_near, 1)
        decode_later(c, 1)
        earlier(2, give, 0)
        decode_own(c, 0)
        earlier(1, send_far, 0)
        decode_own(c, 1)

        @pl.when(c < chunks - 1)
        def _():
            for t in range(tiles):
                encode(c + 1, t)
                if t == 0:
                    send_near(c, 0)

            @pl.when(c >= 1)
            def _():
                send_far(c - 1, 1)

    last = chunks - 1
    tail = []
    for c in range(chunks):
        for h in range(PIECES):
            base = 7.0 * c + 3.1 * h
            if c == last:
                tail.append((base + 8.6, send_near, c, h))
            if (h == 0 and c == last) or (h == 1 and c >= last - 1):
                tail.append((base + 13.1, send_far, c, h))
            if h == 1 or c >= last - 1:
                tail.append((base + 17.6, give, c, h))
            tail.append((base + 22.1, pass_near, c, h))
            tail.append((base + 26.6, pass_down, c, h))
        tail.append((7.0 * c + 35.0, lambda c, h: gradient(c), c, 0))
    for _, action, c, h in sorted(tail, key=lambda e: e[0]):
        action(c, h)

    @pl.loop(0, chunks)
    def _(c):
        for h in range(PIECES):
            @pl.when(layer < layers - 1)
            def _():
                up(c, h).wait_send()

            for q in range(1, m):
                add_near(c, h, q).wait_send()
                give_near(c, h, q, x).wait_send()
            for r in range(1, o):
                add_far(c, h, r).wait_send()
                give_far(c, h, r, z).wait_send()

            @pl.when(layer > 0)
            def _():
                for q in range(m):
                    down(c, h, q).wait_send()


def step(layers, n, acts, enc, dec, enc_bias, targets, bias):
    o, m, chunks, rows, width = acts.shape
    features = enc.shape[1]
    block = n * rows
    half, full = jnp.bfloat16, jnp.float32
    vmem = pl.BlockSpec(memory_space=pltpu.VMEM)
    anywhere = pl.BlockSpec(memory_space=pl.ANY)
    dma = pltpu.SemaphoreType.DMA
    parts = features // 256 if features % 256 == 0 else 1
    pairs = [(), (m - 1,), (o - 1,), (o - 1,), (m - 1,), (m,)]
    return pl.pallas_call(
        functools.partial(step_kernel, layers, m, o),
        out_shape=(
            jax.ShapeDtypeStruct((chunks, rows, width), full),
            jax.ShapeDtypeStruct((chunks, block, features), half),
            jax.ShapeDtypeStruct((chunks, m, o, rows, width), half),
        ),
        in_specs=[anywhere, anywhere, anywhere, vmem, vmem, vmem],
        out_specs=(vmem, vmem, vmem),
        scratch_shapes=[
            pltpu.VMEM((width, features), half),
            pltpu.VMEM((features, 2, width), half),
            pltpu.VMEM((2, features, width), half),
            pltpu.VMEM((chunks, block, features), full),
            pltpu.VMEM((block, features), half),
            pltpu.VMEM((2, block, width), full),
            pltpu.VMEM((chunks, block, width), half),
            pltpu.VMEM((chunks, block, width), half),
            pltpu.VMEM((chunks, m, o, rows, width), half),
            pltpu.VMEM((chunks, m - 1, o, rows, width), half),
            pltpu.VMEM((chunks, o, rows, width), half),
            pltpu.VMEM((chunks, o - 1, rows, width), half),
            pltpu.VMEM((chunks, m, o, rows, width), half),
            pltpu.VMEM((chunks, m, o, rows, width), half),
            dma((chunks, m)),
            dma((features // tile_of(features),)),
            dma((parts,)),
            *[dma((chunks, PIECES, *p)) for p in pairs for _ in range(2)],
        ],
        compiler_params=pltpu.CompilerParams(
            collective_id=0, has_side_effects=True, vmem_limit_bytes=58 * 2**20
        ),
        name="step",
    )(acts, enc, dec, enc_bias, targets, bias)


def weigh_kernel(scale, acts_ref, grad_ref, out_ref):
    total = lax.dot_general(
        acts_ref[...], grad_ref[...], (((0,), (0,)), ((), ())), preferred_element_type=jnp.float32
    )
    out_ref[...] = (total * scale).astype(jnp.bfloat16)


def encoder_grad(acts, grad):
    tokens, features = grad.shape
    width = acts.shape[1]
    tile = 512 if features % 512 == 0 else 256
    return pl.pallas_call(
        functools.partial(weigh_kernel, tokens ** (-0.5)),
        grid=(features // tile,),
        out_shape=jax.ShapeDtypeStruct((width, features), jnp.bfloat16),
        in_specs=[
            pl.BlockSpec(memory_space=pltpu.VMEM),
            pl.BlockSpec((tokens, tile), lambda i: (0, i)),
        ],
        out_specs=pl.BlockSpec((width, tile), lambda i: (0, i)),
        compiler_params=pltpu.CompilerParams(vmem_limit_bytes=24 * 2**20),
        name="encoder_grad",
    )(acts, grad)


def local(layers, n, acts, targets, enc_weight, enc_bias, dec_weight, dec_bias):
    tokens, width = acts.shape[1:]
    m = inner_of(n)
    rows = tokens // n
    chunks = chunks_of(rows)
    errors, grad, turned = step(
        layers, n,
        acts.reshape(n // m, m, chunks, rows // chunks, width),
        enc_weight[0], dec_weight[0], enc_bias,
        targets.reshape(chunks, rows // chunks, width), dec_bias,
    )
    enc_grad = encoder_grad(turned.reshape(tokens, width), grad.reshape(tokens, -1))
    return (errors.reshape(1, rows, width), enc_grad[None])


def solution(mesh):
    return jax.shard_map(
        functools.partial(local, mesh.shape["layer"], mesh.shape["feat"]),
        mesh=mesh,
        in_specs=(
            P("layer", None, None),
            P("layer", "feat", None),
            P("layer", None, "feat"),
            P("layer", "feat"),
            P("layer", "feat", None, None),
            P("layer", None),
        ),
        out_specs=(P("layer", "feat", None), P("layer", None, "feat")),
        check_vma=False,
    )
```

time: 127 us -> 88.8 us (0.70)
  matrix products: 15.9 us -> 0 us
  Pallas kernels: 97.3 us -> 83.7 us
  local copies, waits for them, and re-layouts: 12.1 us -> 4.26 us
    dot_general x1 -> x0, matrix products: 15.9 us -> none  [local(): pre = jnp.dot(inputs, weight, preferred_element_type=jnp.float32) + bias]
    pallas_call x2, Pallas kernels: 97.3 us -> 83.7 us  [the longest x1 77.3 us: step(): pl.pallas_call(functools.partial(step_kernel, layers, m, o), out_shape=(j...]
    unnamed x8 -> x7, local copies, waits for them, and re-layouts: 12.1 us -> 4.26 us
where the time goes in v1:
time: 88.8 us; the launch traced here: 88.6 us
  Pallas kernels  83.7 us (94%)
  local copies, waits for them, and re-layouts  4.26 us (5%)
    pallas_call x1, Pallas kernels, step(): pl.pallas_call(functools.partial(step_kernel, layers, m, o), out_shape=(j...  77.3 us
    pallas_call x1, Pallas kernels, encoder_grad(): pl.pallas_call(functools.partial(weigh_kernel, tokens ** (-0.5)), grid=(f...  6.37 us
    unnamed x7, local copies, waits for them, and re-layouts  4.26 us

profile of v1, /device:TPU:1, one launch (start us, length us, event | category | flops | bytes accessed | tf_op | source)
XLA Modules:
  0.0 88.6 jit_solution(12926542290974683376)
XLA Ops:
  0.6 77.3 %step.1 = (f32[3,32,1024]{2,1,0:T(8,128)}, bf16[3,256,2560]{2,1,0:T(8,128)(2,1)}, bf16[3,2,4,32,1024]{4,3,2,1,0:T(8,128)(2,1)}) custom-call(bf16[4,2,3,32,1024]{4,3,2,1,0:T(8,128)(2,1)} %bitcast.13, bf16[1024,2560]{1,0:T(8,128)(2,1)} %bitcast.11, bf16[2560,2,1024]{2,1,0:T(2,128)(2,1)} %bitcast.10, f32[1,2560]{1,0:T(1,128)} %enc_bias_ref.1, ...), custom_call_target="tpu_custom_call" | custom-call | tf_op jit(solution)/shard_map/step/pallas_call | solution.py:312
  77.9 0.0 copy-start
  77.9 2.1 %copy-done = bf16[3,256,2560]{2,1,0:T(8,128)(2,1)S(1)} copy-done((bf16[3,256,2560]{2,1,0:T(8,128)(2,1)S(1)}, bf16[3,256,2560]{2,1,0:T(8,128)(2,1)}, u32[]{:S(2)}) %copy-start) | copy-done | bytes 3932184
  80.0 0.0 copy-start.1
  80.1 1.4 %copy-done.1 = bf16[3,2,4,32,1024]{4,3,2,1,0:T(8,128)(2,1)S(1)} copy-done((bf16[3,2,4,32,1024]{4,3,2,1,0:T(8,128)(2,1)S(1)}, bf16[3,2,4,32,1024]{4,3,2,1,0:T(8,128)(2,1)}, u32[]{:S(2)}) %copy-start.1) | copy-done | bytes 1572888
  81.5 0.0 copy-start.2
  81.5 6.4 %encoder_grad.1 = bf16[1024,2560]{1,0:T(8,128)(2,1)} custom-call(bf16[768,1024]{1,0:T(8,128)(2,1)S(1)} %bitcast.9, bf16[768,2560]{1,0:T(8,128)(2,1)S(1)} %bitcast.8), custom_call_target="tpu_custom_call" | custom-call | tf_op jit(solution)/shard_map/encoder_grad/pallas_call | solution.py:359
  87.8 0.0 copy-done.2
  87.8 0.7 copy.9
Async XLA Ops:
  77.9 2.1 %copy-start = (bf16[3,256,2560]{2,1,0:T(8,128)(2,1)S(1)}, bf16[3,256,2560]{2,1,0:T(8,128)(2,1)}, u32[]{:S(2)}) copy-start(bf16[3,256,2560]{2,1,0:T(8,128)(2,1)} %get-tuple-element.7) | copy-start | bytes 11796484
  80.0 1.4 %copy-start.1 = (bf16[3,2,4,32,1024]{4,3,2,1,0:T(8,128)(2,1)S(1)}, bf16[3,2,4,32,1024]{4,3,2,1,0:T(8,128)(2,1)}, u32[]{:S(2)}) copy-start(bf16[3,2,4,32,1024]{4,3,2,1,0:T(8,128)(2,1)} %get-tuple-element.6) | copy-start | bytes 4718596
  81.5 6.4 %copy-start.2 = (f32[3,32,1024]{2,1,0:T(8,128)S(1)}, f32[3,32,1024]{2,1,0:T(8,128)}, u32[]{:S(2)}) copy-start(f32[3,32,1024]{2,1,0:T(8,128)} %get-tuple-element.5) | copy-start | bytes 1179652

commit v2 on v1

v2 whole, which is shorter than its diff:
```python
import functools

import jax
import jax.numpy as jnp
from jax import lax
from jax.experimental import pallas as pl
from jax.experimental.pallas import tpu as pltpu
from jax.sharding import PartitionSpec as P

MESH = pl.DeviceIdType.MESH
PIECES = 4
DOTS = 2


def inner_of(n):
    return max(d for d in range(1, n + 1) if n % d == 0 and d * d <= n)


def chunks_of(rows):
    return next((c for c in (3, 2) if rows % (16 * c) == 0), 1)


def tile_of(features):
    return features // 2 if features % 256 == 0 else features


def contract_width(errs, decoder):
    return lax.dot_general(
        errs, decoder, (((1,), (1,)), ((), ())), preferred_element_type=jnp.float32
    )


def plan(chunks):
    places = {
        "x": ((3, 0), (4, 0), (5, 0), (0, 1)), "low": ((0, 1), (1, 1), (3, 1), (4, 1)),
        "high": ((3, 1), (4, 1), (5, 1), (0, 2)), "give_high": ((5, 1), (0, 2), (2, 2), (3, 2)),
        "give_low": ((2, 2), (3, 2), (4, 2), (5, 2)), "give_x": ((4, 2), (5, 2), (5, 2), (5, 2)),
        "down": ((5, 3), (5, 3), (5, 3), (5, 3)),
    }
    points = (0.85, 1.7, 2.55, 3.4, 5.0, 6.6)
    period = 6.6
    queued = {"down": (21.4, 22.9, 24.4, 25.9)}
    inside, rest = [[] for _ in points], []
    for stage, spots in places.items():
        for h, (spot, back) in enumerate(spots):
            when = points[spot] + back * period
            inside[spot].append((when, back, stage, h))
            final = chunks - 1 if spot < 4 else chunks - 2
            for c in range(chunks):
                if c + back > final:
                    late = queued.get(stage, spots)[h] if stage in queued else when
                    rest.append((c * period + late, stage, c, h))
    for spot in inside:
        spot.sort(key=lambda e: -e[0])
    return inside, rest


def step_kernel(
    layers, m, lo, hi, scale, acts_hbm, enc_hbm, dec_hbm, enc_bias_ref, targets_ref, bias_ref,
    errors_ref, enc,
    acts, raw, dec, deriv, latent, own, total, later, arrived, sums, near, low_in, high_in, gath, foll,
    acts_sem, enc_sem, dec_sem, up_send, up_recv, x_send, x_recv, low_send, low_recv, high_send, high_recv,
    ghigh_send, ghigh_recv, glow_send, glow_recv, gx_send, gx_recv, down_send, down_recv,
):
    layer = lax.axis_index("layer")
    me = lax.axis_index("feat")
    x = lax.rem(me, m)
    zl, zh = lax.rem(me // m, lo), me // (m * lo)
    above = lax.rem(layer + 1, layers)
    below = lax.rem(layer + layers - 1, layers)
    chunks, rows, width = later.shape[0], *later.shape[4:]
    block = m * lo * hi * rows
    features = enc.shape[1]
    tile = tile_of(features)
    tiles = features // tile
    slots, raws = raw.shape[:2]
    parts = features // raws
    wide = width // PIECES
    dot = width // DOTS

    def at(h, l, xx):
        return (lax.rem(h, hi) * lo + lax.rem(l, lo)) * m + lax.rem(xx, m)

    def cols(h):
        return pl.ds(h * wide, wide)

    def dots(d):
        return pl.ds(d * dot, dot)

    def feats(t):
        return pl.ds(pl.multiple_of(t * tile, tile), tile)

    def remote(src, dst, send, recv, where):
        return pltpu.make_async_remote_copy(
            src_ref=src, dst_ref=dst, send_sem=send, recv_sem=recv,
            device_id=where, device_id_type=MESH,
        )

    def load_acts(c, q, l):
        return pltpu.make_async_copy(acts_hbm.at[:, l, q, c], acts.at[c, q, l], acts_sem.at[c, q, l])

    def load_enc(t):
        return pltpu.make_async_copy(enc_hbm.at[:, feats(t)], enc.at[:, feats(t)], enc_sem.at[t])

    def load_dec(i):
        part = pl.ds(pl.multiple_of(i * raws, raws), raws)
        return pltpu.make_async_copy(dec_hbm.at[part], raw.at[lax.rem(i, slots)], dec_sem.at[i])

    def up(c, h):
        return remote(
            later.at[c, :, :, :, :, cols(h)], arrived.at[c, :, :, :, :, cols(h)],
            up_send.at[c, h], up_recv.at[c, h], (above, me),
        )

    def add_x(c, h, q):
        to = lax.rem(x + q, m)
        return remote(
            sums.at[c, to, :, :, :, cols(h)], near.at[c, q - 1, :, :, :, cols(h)],
            x_send.at[c, h, q - 1], x_recv.at[c, h, q - 1], (layer, at(zh, zl, to)),
        )

    def add_low(c, h, q):
        to = lax.rem(zl + q, lo)
        return remote(
            later.at[c, 0, to, :, :, cols(h)], low_in.at[c, q - 1, :, :, cols(h)],
            low_send.at[c, h, q - 1], low_recv.at[c, h, q - 1], (layer, at(zh, to, x)),
        )

    def add_high(c, h, q):
        to = lax.rem(zh + q, hi)
        return remote(
            later.at[c, 0, zl, to, :, cols(h)], high_in.at[c, q - 1, :, cols(h)],
            high_send.at[c, h, q - 1], high_recv.at[c, h, q - 1], (layer, at(to, zl, x)),
        )

    def give_high(c, h, q, owner):
        spot = gath.at[c, x, zl, owner, :, cols(h)]
        return remote(
            spot, spot, ghigh_send.at[c, h, q - 1], ghigh_recv.at[c, h, q - 1], (layer, at(zh + q, zl, x))
        )

    def give_low(c, h, q, owner):
        spot = gath.at[c, x, owner, :, :, cols(h)]
        return remote(
            spot, spot, glow_send.at[c, h, q - 1], glow_recv.at[c, h, q - 1], (layer, at(zh, zl + q, x))
        )

    def give_x(c, h, q, owner):
        spot = gath.at[c, owner, :, :, :, cols(h)]
        return remote(
            spot, spot, gx_send.at[c, h, q - 1], gx_recv.at[c, h, q - 1], (layer, at(zh, zl, x + q))
        )

    def down(c, h, q):
        owner = lax.rem(x + m - q, m)
        return remote(
            gath.at[c, owner, :, :, :, cols(h)], foll.at[c, owner, :, :, :, cols(h)],
            down_send.at[c, h, q], down_recv.at[c, h, q], (below, me),
        )

    def encode(c, t):
        lhs = acts[c].reshape(block, width)
        pre = jnp.dot(lhs, enc[:, feats(t)], preferred_element_type=jnp.float32)
        scaled = 4.0 * (pre + enc_bias_ref[:, feats(t)])
        shrunk = jnp.exp(-jnp.abs(scaled))
        latent[:, feats(t)] = ((jnp.maximum(scaled, 0.0) + jnp.log1p(shrunk)) * 0.25).astype(jnp.bfloat16)
        part = 1.0 / (1.0 + shrunk)
        deriv[c, :, feats(t)] = jnp.where(scaled >= 0.0, part, shrunk * part).astype(jnp.bfloat16)

    def decode_later(c, d):
        value = jnp.dot(latent[...], dec[1, :, dots(d)], preferred_element_type=jnp.float32)
        later[c, :, :, :, :, dots(d)] = value.astype(jnp.bfloat16).reshape(m, lo, hi, rows, dot)

        @pl.when(layer < layers - 1)
        def _():
            for h in range(d * PIECES // DOTS, (d + 1) * PIECES // DOTS):
                up(c, h).start()

    def decode_own(c, d):
        own[:, dots(d)] = jnp.dot(
            latent[...], dec[0, :, dots(d)], preferred_element_type=jnp.float32
        )

    def send_x(c, h):
        @pl.when(layer > 0)
        def _():
            up(c, h).wait_recv()

        carried = jnp.where(layer > 0, arrived[c, :, :, :, :, cols(h)].reshape(block, wide).astype(jnp.float32), 0.0)
        both = (own[:, cols(h)] + carried).astype(jnp.bfloat16)
        sums[c, :, :, :, :, cols(h)] = both.reshape(m, lo, hi, rows, wide)
        for q in range(1, m):
            add_x(c, h, q).start()

    def send_low(c, h):
        value = sums[c, x, :, :, :, cols(h)].astype(jnp.float32)
        for q in range(1, m):
            add_x(c, h, q).wait_recv()
            value = value + near[c, q - 1, :, :, :, cols(h)].astype(jnp.float32)

        @pl.when(layer < layers - 1)
        def _():
            up(c, h).wait_send()

        later[c, 0, :, :, :, cols(h)] = value.astype(jnp.bfloat16)
        for q in range(1, lo):
            add_low(c, h, q).start()

    def own_low(c, h, spot):
        value = sums[c, x, zl, spot, :, cols(h)].astype(jnp.float32)
        for q in range(1, m):
            value = value + near[c, q - 1, zl, spot, :, cols(h)].astype(jnp.float32)
        for q in range(1, lo):
            value = value + low_in[c, q - 1, spot, :, cols(h)].astype(jnp.float32)
        return value

    def send_high(c, h):
        for q in range(1, lo):
            add_low(c, h, q).wait_recv()
        for q in range(1, hi):
            to = lax.rem(zh + q, hi)
            later[c, 0, zl, to, :, cols(h)] = own_low(c, h, to).astype(jnp.bfloat16)
            add_high(c, h, q).start()

    def send_errors(c, h):
        value = own_low(c, h, zh)
        for q in range(1, hi):
            add_high(c, h, q).wait_recv()
            value = value + high_in[c, q - 1, :, cols(h)].astype(jnp.float32)
        errors = value + bias_ref[:, cols(h)] - targets_ref[c, :, cols(h)].astype(jnp.float32)
        errors_ref[c, :, cols(h)] = errors
        gath[c, x, zl, zh, :, cols(h)] = errors.astype(jnp.bfloat16)
        for q in range(1, hi):
            give_high(c, h, q, zh).start()

    def pass_low(c, h):
        for q in range(1, hi):
            give_high(c, h, q, lax.rem(zh + hi - q, hi)).wait_recv()
        for q in range(1, lo):
            give_low(c, h, q, zl).start()

    def pass_x(c, h):
        for q in range(1, lo):
            give_low(c, h, q, lax.rem(zl + lo - q, lo)).wait_recv()
        for q in range(1, m):
            give_x(c, h, q, x).start()

        @pl.when(layer > 0)
        def _():
            down(c, h, 0).start()

    def pass_down(c, h):
        for q in range(1, m):
            give_x(c, h, q, lax.rem(x + m - q, m)).wait_recv()

        @pl.when(layer > 0)
        def _():
            for q in range(1, m):
                down(c, h, q).start()

    def gradient(c, t):
        if t == 0:
            @pl.when(layer < layers - 1)
            def _():
                for h in range(PIECES):
                    for q in range(m):
                        down(c, h, q).wait_recv()

        grad = contract_width(gath[c].reshape(block, width), dec[0, feats(t), :])
        grad = grad + contract_width(foll[c].reshape(block, width), dec[1, feats(t), :])
        latent[:, feats(t)] = (grad * deriv[c, :, feats(t)].astype(jnp.float32)).astype(jnp.bfloat16)

    def weigh(c, t):
        value = lax.dot_general(
            acts[c].reshape(block, width), latent[:, feats(t)], (((0,), (0,)), ((), ())),
            preferred_element_type=jnp.float32,
        )
        if c > 0:
            value = total[:, feats(t)] + value
        if c < chunks - 1:
            total[:, feats(t)] = value
        else:
            enc[:, feats(t)] = (value * scale).astype(jnp.bfloat16)

    run = {
        "x": send_x, "low": send_low, "high": send_high, "give_high": send_errors,
        "give_low": pass_low, "give_x": pass_x, "down": pass_down, "gradient": gradient, "weigh": weigh,
    }
    inside, rest = plan(chunks)

    def every(c):
        return [load_acts(c, q, l) for q in range(m) for l in range(lo)]

    for copy in every(0):
        copy.start()
    for t in range(tiles):
        load_enc(t).start()

    @pl.when(layer == layers - 1)
    def _():
        foll[...] = jnp.zeros_like(foll)

    barrier = pltpu.get_barrier_semaphore()
    for to in (
        [(layer, at(zh, zl, x + q)) for q in range(1, m)]
        + [(layer, at(zh, zl + q, x)) for q in range(1, lo)]
        + [(layer, at(zh + q, zl, x)) for q in range(1, hi)]
        + [(above, me), (below, me)]
    ):
        pl.semaphore_signal(barrier, inc=1, device_id=to, device_id_type=MESH)

    for copy in every(0):
        copy.wait()
    load_enc(0).wait()
    for i in range(slots):
        load_dec(i).start()
    for c in range(1, chunks):
        for copy in every(c):
            copy.start()

    def split_dec(i):
        load_dec(i).wait()
        dec[:, pl.ds(pl.multiple_of(i * raws, raws), raws), :] = jnp.transpose(raw[lax.rem(i, slots)], (1, 0, 2))

        @pl.when(i + slots < parts)
        def _():
            load_dec(i + slots).start()

    encode(0, 0)
    pl.loop(0, slots)(split_dec)
    for t in range(1, tiles):
        load_enc(t).wait()
        encode(0, t)
    pl.loop(slots, parts)(split_dec)

    for c in range(1, chunks):
        for copy in every(c):
            copy.wait()

    pl.semaphore_wait(barrier, m + lo + hi - 1)

    @pl.loop(0, chunks)
    def _(c):
        def attend(spot):
            for _, back, stage, h in inside[spot]:
                @pl.when(c >= back)
                def _():
                    run[stage](c - back, h)

        decode_later(c, 0)
        attend(0)
        decode_later(c, 1)
        attend(1)
        decode_own(c, 0)
        attend(2)
        decode_own(c, 1)
        attend(3)

        @pl.when(c < chunks - 1)
        def _():
            for t in range(tiles):
                encode(c + 1, t)
                if t < 2:
                    attend(4 + t)

    for c in range(chunks):
        base = 6.6 * c + 28.0
        for t in range(tiles):
            rest.append((base + 1.6 * t, "gradient", c, t))
            rest.append((base + 3.2 + 1.0 * t, "weigh", c, t))
    for _, stage, c, k in sorted(rest, key=lambda e: e[0]):
        run[stage](c, k)

    @pl.loop(0, chunks)
    def _(c):
        for h in range(PIECES):
            for q in range(1, m):
                add_x(c, h, q).wait_send()
                give_x(c, h, q, x).wait_send()
            for q in range(1, lo):
                add_low(c, h, q).wait_send()
                give_low(c, h, q, zl).wait_send()
            for q in range(1, hi):
                add_high(c, h, q).wait_send()
                give_high(c, h, q, zh).wait_send()

            @pl.when(layer > 0)
            def _():
                for q in range(m):
                    down(c, h, q).wait_send()


def step(layers, tokens, acts, enc, dec, enc_bias, targets, bias):
    hi, lo, m, chunks, rows, width = acts.shape
    features = enc.shape[1]
    block = tokens // chunks
    half, full = jnp.bfloat16, jnp.float32
    vmem = pl.BlockSpec(memory_space=pltpu.VMEM)
    anywhere = pl.BlockSpec(memory_space=pl.ANY)
    dma = pltpu.SemaphoreType.DMA
    raws = 256
    parts = features // raws
    slots = -(-parts // 2)
    pairs = [(), (m - 1,), (lo - 1,), (hi - 1,), (hi - 1,), (lo - 1,), (m - 1,), (m,)]
    return pl.pallas_call(
        functools.partial(step_kernel, layers, m, lo, hi, tokens ** (-0.5)),
        out_shape=(
            jax.ShapeDtypeStruct((chunks, rows, width), full),
            jax.ShapeDtypeStruct((width, features), half),
        ),
        in_specs=[anywhere, anywhere, anywhere, vmem, vmem, vmem],
        out_specs=(vmem, vmem),
        scratch_shapes=[
            pltpu.VMEM((chunks, m, lo, hi, rows, width), half),
            pltpu.VMEM((slots, raws, 2, width), half),
            pltpu.VMEM((2, features, width), half),
            pltpu.VMEM((chunks, block, features), half),
            pltpu.VMEM((block, features), half),
            pltpu.VMEM((block, width), full),
            pltpu.VMEM((width, features), full),
            pltpu.VMEM((chunks, m, lo, hi, rows, width), half),
            pltpu.VMEM((chunks, m, lo, hi, rows, width), half),
            pltpu.VMEM((chunks, m, lo, hi, rows, width), half),
            pltpu.VMEM((chunks, m - 1, lo, hi, rows, width), half),
            pltpu.VMEM((chunks, lo - 1, hi, rows, width), half),
            pltpu.VMEM((chunks, hi - 1, rows, width), half),
            pltpu.VMEM((chunks, m, lo, hi, rows, width), half),
            pltpu.VMEM((chunks, m, lo, hi, rows, width), half),
            dma((chunks, m, lo)),
            dma((features // tile_of(features),)),
            dma((parts,)),
            *[dma((chunks, PIECES, *p)) for p in pairs for _ in range(2)],
        ],
        compiler_params=pltpu.CompilerParams(
            collective_id=0, has_side_effects=True, vmem_limit_bytes=46 * 2**20
        ),
        name="step",
    )(acts, enc, dec, enc_bias, targets, bias)


def local(layers, n, acts, targets, enc_weight, enc_bias, dec_weight, dec_bias):
    tokens, width = acts.shape[1:]
    m = inner_of(n)
    lo = inner_of(n // m)
    rows = tokens // n
    chunks = chunks_of(rows)
    errors, enc_grad = step(
        layers, tokens,
        acts.reshape(n // (m * lo), lo, m, chunks, rows // chunks, width),
        enc_weight[0], dec_weight[0], enc_bias,
        targets.reshape(chunks, rows // chunks, width), dec_bias,
    )
    return (errors.reshape(1, rows, width), enc_grad[None])


def solution(mesh):
    return jax.shard_map(
        functools.partial(local, mesh.shape["layer"], mesh.shape["feat"]),
        mesh=mesh,
        in_specs=(
            P("layer", None, None),
            P("layer", "feat", None),
            P("layer", None, "feat"),
            P("layer", "feat"),
            P("layer", "feat", None, None),
            P("layer", None),
        ),
        out_specs=(P("layer", "feat", None), P("layer", None, "feat")),
        check_vma=False,
    )
```

time: 88.8 us -> 82.4 us (0.928)
  Pallas kernels: 83.7 us -> 74.7 us
  local copies, waits for them, and re-layouts: 4.26 us -> 6.82 us
    pallas_call x2 -> x1, Pallas kernels: 83.7 us -> 74.7 us  [step(): pl.pallas_call(functools.partial(step_kernel, layers, m, lo, hi, tokens *...]
    unnamed x7 -> x10, local copies, waits for them, and re-layouts: 4.26 us -> 6.82 us
where the time goes in v2:
time: 82.4 us; the launch traced here: 82.2 us
  Pallas kernels  74.7 us (91%)
  local copies, waits for them, and re-layouts  6.82 us (8%)
    pallas_call x1, Pallas kernels, step(): pl.pallas_call(functools.partial(step_kernel, layers, m, lo, hi, tokens *...  74.7 us
    unnamed x10, local copies, waits for them, and re-layouts  6.82 us

profile of v2, /device:TPU:1, one launch (start us, length us, event | category | flops | bytes accessed | tf_op | source)
XLA Modules:
  0.0 82.2 jit_solution(16814383359705158389)
XLA Ops:
  0.6 0.0 copy-start
  0.6 1.4 %copy-done = bf16[1,768,1024]{2,1,0:T(8,128)(2,1)S(1)} copy-done((bf16[1,768,1024]{2,1,0:T(8,128)(2,1)S(1)}, bf16[1,768,1024]{2,1,0:T(8,128)(2,1)}, u32[]{:S(2)}) %copy-start) | copy-done | bytes 1572888
  2.0 0.0 copy-start.1
  2.0 0.9 %copy-done.1 = bf16[1,96,1024]{2,1,0:T(8,128)(2,1)S(1)} copy-done((bf16[1,96,1024]{2,1,0:T(8,128)(2,1)S(1)}, bf16[1,96,1024]{2,1,0:T(8,128)(2,1)}, u32[]{:S(2)}) %copy-start.1) | copy-done | bytes 196632
  3.0 0.0 copy-start.2
  3.0 0.7 copy-done.2
  3.7 0.0 copy-start.3
  3.7 0.7 copy-done.3
  4.4 74.7 %step.1 = (f32[3,32,1024]{2,1,0:T(8,128)S(1)}, bf16[1024,2560]{1,0:T(8,128)(2,1)S(1)}) custom-call(bf16[2,2,2,3,32,1024]{5,4,3,2,1,0:T(8,128)(2,1)S(1)} %bitcast.7, bf16[1024,2560]{1,0:T(8,128)(2,1)} %bitcast.11, bf16[2560,2,1024]{2,1,0:T(2,128)(2,1)} %bitcast.10, f32[1,2560]{1,0:T(1,128)S(1)} %copy-done.2, bf16[3,32,1024]{2,1,0:T(8,128)(2,1)S(1)} %bitcast.9, ...), custom_call_target="tpu_custom_call" | custom-call | tf_op jit(solution)/shard_map/step/pallas_call | solution.py:405
  79.1 0.7 copy.10
  79.8 2.4 %copy.11 = bf16[1,1024,2560]{2,1,0:T(8,128)(2,1)} copy(bf16[1,1024,2560]{2,1,0:T(8,128)(2,1)S(1)} %bitcast.6) | data formatting | bytes 10485760
Async XLA Ops:
  0.6 1.4 %copy-start = (bf16[1,768,1024]{2,1,0:T(8,128)(2,1)S(1)}, bf16[1,768,1024]{2,1,0:T(8,128)(2,1)}, u32[]{:S(2)}) copy-start(bf16[1,768,1024]{2,1,0:T(8,128)(2,1)} %param.6) | copy-start | bytes 4718596
  2.0 0.9 %copy-start.1 = (bf16[1,96,1024]{2,1,0:T(8,128)(2,1)S(1)}, bf16[1,96,1024]{2,1,0:T(8,128)(2,1)}, u32[]{:S(2)}) copy-start(bf16[1,96,1024]{2,1,0:T(8,128)(2,1)} %param.7) | copy-start | bytes 589828
  3.0 0.7 copy-start.2
  3.7 0.7 copy-start.3

commit v3 on v2

--- a/solution.py
+++ b/solution.py
@@ -30,37 +30,52 @@
     )
 
 
-def plan(chunks):
-    places = {
-        "x": ((3, 0), (4, 0), (5, 0), (0, 1)), "low": ((0, 1), (1, 1), (3, 1), (4, 1)),
-        "high": ((3, 1), (4, 1), (5, 1), (0, 2)), "give_high": ((5, 1), (0, 2), (2, 2), (3, 2)),
-        "give_low": ((2, 2), (3, 2), (4, 2), (5, 2)), "give_x": ((4, 2), (5, 2), (5, 2), (5, 2)),
-        "down": ((5, 3), (5, 3), (5, 3), (5, 3)),
-    }
-    points = (0.85, 1.7, 2.55, 3.4, 5.0, 6.6)
-    period = 6.6
-    queued = {"down": (21.4, 22.9, 24.4, 25.9)}
-    inside, rest = [[] for _ in points], []
-    for stage, spots in places.items():
-        for h, (spot, back) in enumerate(spots):
-            when = points[spot] + back * period
-            inside[spot].append((when, back, stage, h))
+SPOTS = {
+    "x": (3, 4, 6, 6),
+    "low": (5, 7, 10, 10),
+    "high": (8, 10, 12, 12),
+    "give_z": (11, 13, 15, 15),
+    "give_x": (15, 21, 23, 18),
+    "down": (28, 23, 29, 24),
+}
+REST = {
+    "x": ((0, 0, 0, 0), (0, 0, 0, 0), (0, 1, 2, 0)),
+    "low": ((0, 0, 0, 0), (0, 0, 4, 3), (6, 10, 9, 20)),
+    "high": ((0, 0, 0, 0), (0, 5, 7, 11), (18, 26, 25, 38)),
+    "give_z": ((0, 0, 0, 0), (8, 12, 19, 27), (30, 36, 41, 47)),
+    "give_x": ((0, 16, 17, 22), (33, 28, 40, 35), (55, 51, 54, 58)),
+    "down": ((32, 23, 24, 31), (44, 43, 50, 49), (61, 57, 60, 63)),
+    "gradient": ((34, 42), (56, 59), (65, 66)),
+    "weigh": ((46, 52), (62, 64), (67, 68)),
+}
+
+
+def plan(chunks, tiles):
+    inside, rest = [[] for _ in range(6)], []
+    ends = len(REST["x"])
+
+    def rank(stage, c, k):
+        rows = REST[stage]
+        return (rows[max(0, min(c, ends - 1 - (chunks - 1 - c)))][k], c)
+
+    for stage, spots in SPOTS.items():
+        for h, place in enumerate(spots):
+            back, spot = divmod(place, 6)
+            inside[spot].append((back, stage, h))
             final = chunks - 1 if spot < 4 else chunks - 2
-            for c in range(chunks):
-                if c + back > final:
-                    late = queued.get(stage, spots)[h] if stage in queued else when
-                    rest.append((c * period + late, stage, c, h))
+            rest += [(stage, c, h) for c in range(chunks) if c + back > final]
     for spot in inside:
         spot.sort(key=lambda e: -e[0])
-    return inside, rest
+    rest += [(stage, c, t) for c in range(chunks) for stage in ("gradient", "weigh") for t in range(tiles)]
+    return inside, sorted(rest, key=lambda e: rank(*e))
 
 
 def step_kernel(
-    layers, m, lo, hi, scale, acts_hbm, enc_hbm, dec_hbm, enc_bias_ref, targets_ref, bias_ref,
+    layers, m, lo, hi, scale, acts_hbm, enc_hbm, dec_hbm, enc_bias_hbm, targets_hbm, bias_hbm,
     errors_ref, enc,
-    acts, raw, dec, deriv, latent, own, total, later, arrived, sums, near, low_in, high_in, gath, foll,
-    acts_sem, enc_sem, dec_sem, up_send, up_recv, x_send, x_recv, low_send, low_recv, high_send, high_recv,
-    ghigh_send, ghigh_recv, glow_send, glow_recv, gx_send, gx_recv, down_send, down_recv,
+    enc_bias_ref, targets_ref, bias_ref, acts, raw, dec, deriv, latent, own, total, later, arrived, sums, near, low_in, high_in, gath, foll,
+    small_sem, acts_sem, enc_sem, dec_sem, up_send, up_recv, x_send, x_recv, low_send, low_recv, high_send, high_recv,
+    gz_send, gz_recv, gx_send, gx_recv, down_send, down_recv,
 ):
     layer = lax.axis_index("layer")
     me = lax.axis_index("feat")
@@ -75,6 +90,7 @@
     tiles = features // tile
     slots, raws = raw.shape[:2]
     parts = features // raws
+    deep, mine = lo * hi, zl * hi + zh
     wide = width // PIECES
     dot = width // DOTS
 
@@ -133,16 +149,11 @@
             high_send.at[c, h, q - 1], high_recv.at[c, h, q - 1], (layer, at(to, zl, x)),
         )
 
-    def give_high(c, h, q, owner):
-        spot = gath.at[c, x, zl, owner, :, cols(h)]
-        return remote(
-            spot, spot, ghigh_send.at[c, h, q - 1], ghigh_recv.at[c, h, q - 1], (layer, at(zh + q, zl, x))
-        )
-
-    def give_low(c, h, q, owner):
-        spot = gath.at[c, x, owner, :, :, cols(h)]
-        return remote(
-            spot, spot, glow_send.at[c, h, q - 1], glow_recv.at[c, h, q - 1], (layer, at(zh, zl + q, x))
+    def give_z(c, h, q, owner):
+        spot = gath.at[c, x, owner // hi, lax.rem(owner, hi), :, cols(h)]
+        to = lax.rem(mine + q, deep)
+        return remote(
+            spot, spot, gz_send.at[c, h, q - 1], gz_recv.at[c, h, q - 1], (layer, at(lax.rem(to, hi), to // hi, x))
         )
 
     def give_x(c, h, q, owner):
@@ -230,18 +241,12 @@
         errors = value + bias_ref[:, cols(h)] - targets_ref[c, :, cols(h)].astype(jnp.float32)
         errors_ref[c, :, cols(h)] = errors
         gath[c, x, zl, zh, :, cols(h)] = errors.astype(jnp.bfloat16)
-        for q in range(1, hi):
-            give_high(c, h, q, zh).start()
-
-    def pass_low(c, h):
-        for q in range(1, hi):
-            give_high(c, h, q, lax.rem(zh + hi - q, hi)).wait_recv()
-        for q in range(1, lo):
-            give_low(c, h, q, zl).start()
+        for q in range(1, deep):
+            give_z(c, h, q, mine).start()
 
     def pass_x(c, h):
-        for q in range(1, lo):
-            give_low(c, h, q, lax.rem(zl + lo - q, lo)).wait_recv()
+        for q in range(1, deep):
+            give_z(c, h, q, lax.rem(mine + deep - q, deep)).wait_recv()
         for q in range(1, m):
             give_x(c, h, q, x).start()
 
@@ -283,16 +288,23 @@
             enc[:, feats(t)] = (value * scale).astype(jnp.bfloat16)
 
     run = {
-        "x": send_x, "low": send_low, "high": send_high, "give_high": send_errors,
-        "give_low": pass_low, "give_x": pass_x, "down": pass_down, "gradient": gradient, "weigh": weigh,
+        "x": send_x, "low": send_low, "high": send_high, "give_z": send_errors,
+        "give_x": pass_x, "down": pass_down, "gradient": gradient, "weigh": weigh,
     }
-    inside, rest = plan(chunks)
+    inside, rest = plan(chunks, tiles)
 
     def every(c):
         return [load_acts(c, q, l) for q in range(m) for l in range(lo)]
 
+    small = [
+        pltpu.make_async_copy(source, place, small_sem.at[i])
+        for i, (source, place) in enumerate(
+            ((enc_bias_hbm, enc_bias_ref), (targets_hbm, targets_ref), (bias_hbm, bias_ref))
+        )
+    ]
     for copy in every(0):
         copy.start()
+    small[0].start()
     for t in range(tiles):
         load_enc(t).start()
 
@@ -303,17 +315,19 @@
     barrier = pltpu.get_barrier_semaphore()
     for to in (
         [(layer, at(zh, zl, x + q)) for q in range(1, m)]
-        + [(layer, at(zh, zl + q, x)) for q in range(1, lo)]
-        + [(layer, at(zh + q, zl, x)) for q in range(1, hi)]
+        + [(layer, at(lax.rem(mine + q, hi), lax.rem(mine + q, deep) // hi, x)) for q in range(1, deep)]
         + [(above, me), (below, me)]
     ):
         pl.semaphore_signal(barrier, inc=1, device_id=to, device_id_type=MESH)
 
     for copy in every(0):
         copy.wait()
+    small[0].wait()
     load_enc(0).wait()
     for i in range(slots):
         load_dec(i).start()
+    for copy in small[1:]:
+        copy.start()
     for c in range(1, chunks):
         for copy in every(c):
             copy.start()
@@ -333,16 +347,18 @@
         encode(0, t)
     pl.loop(slots, parts)(split_dec)
 
+    for copy in small[1:]:
+        copy.wait()
     for c in range(1, chunks):
         for copy in every(c):
             copy.wait()
 
-    pl.semaphore_wait(barrier, m + lo + hi - 1)
+    pl.semaphore_wait(barrier, m + deep)
 
     @pl.loop(0, chunks)
     def _(c):
         def attend(spot):
-            for _, back, stage, h in inside[spot]:
+            for back, stage, h in inside[spot]:
                 @pl.when(c >= back)
                 def _():
                     run[stage](c - back, h)
@@ -363,12 +379,7 @@
                 if t < 2:
                     attend(4 + t)
 
-    for c in range(chunks):
-        base = 6.6 * c + 28.0
-        for t in range(tiles):
-            rest.append((base + 1.6 * t, "gradient", c, t))
-            rest.append((base + 3.2 + 1.0 * t, "weigh", c, t))
-    for _, stage, c, k in sorted(rest, key=lambda e: e[0]):
+    for stage, c, k in rest:
         run[stage](c, k)
 
     @pl.loop(0, chunks)
@@ -379,10 +390,10 @@
                 give_x(c, h, q, x).wait_send()
             for q in range(1, lo):
                 add_low(c, h, q).wait_send()
-                give_low(c, h, q, zl).wait_send()
             for q in range(1, hi):
                 add_high(c, h, q).wait_send()
-                give_high(c, h, q, zh).wait_send()
+            for q in range(1, deep):
+                give_z(c, h, q, mine).wait_send()
 
             @pl.when(layer > 0)
             def _():
@@ -396,21 +407,24 @@
     block = tokens // chunks
     half, full = jnp.bfloat16, jnp.float32
     vmem = pl.BlockSpec(memory_space=pltpu.VMEM)
-    anywhere = pl.BlockSpec(memory_space=pl.ANY)
+    outside = pl.BlockSpec(memory_space=pltpu.HBM)
     dma = pltpu.SemaphoreType.DMA
     raws = 256
     parts = features // raws
     slots = -(-parts // 2)
-    pairs = [(), (m - 1,), (lo - 1,), (hi - 1,), (hi - 1,), (lo - 1,), (m - 1,), (m,)]
+    pairs = [(), (m - 1,), (lo - 1,), (hi - 1,), (lo * hi - 1,), (m - 1,), (m,)]
     return pl.pallas_call(
         functools.partial(step_kernel, layers, m, lo, hi, tokens ** (-0.5)),
         out_shape=(
             jax.ShapeDtypeStruct((chunks, rows, width), full),
             jax.ShapeDtypeStruct((width, features), half),
         ),
-        in_specs=[anywhere, anywhere, anywhere, vmem, vmem, vmem],
+        in_specs=[outside] * 6,
         out_specs=(vmem, vmem),
         scratch_shapes=[
+            pltpu.VMEM(enc_bias.shape, full),
+            pltpu.VMEM(targets.shape, half),
+            pltpu.VMEM(bias.shape, full),
             pltpu.VMEM((chunks, m, lo, hi, rows, width), half),
             pltpu.VMEM((slots, raws, 2, width), half),
             pltpu.VMEM((2, features, width), half),
@@ -426,6 +440,7 @@
             pltpu.VMEM((chunks, hi - 1, rows, width), half),
             pltpu.VMEM((chunks, m, lo, hi, rows, width), half),
             pltpu.VMEM((chunks, m, lo, hi, rows, width), half),
+            dma((3,)),
             dma((chunks, m, lo)),
             dma((features // tile_of(features),)),
             dma((parts,)),
@@ -435,7 +450,7 @@
             collective_id=0, has_side_effects=True, vmem_limit_bytes=46 * 2**20
         ),
         name="step",
-    )(acts, enc, dec, enc_bias, targets, bias)
+    )(*[pltpu.with_memory_space_constraint(a, pltpu.HBM) for a in (acts, enc, dec, enc_bias, targets, bias)])
 
 
 def local(layers, n, acts, targets, enc_weight, enc_bias, dec_weight, dec_bias):

time: 82.4 us -> 74.2 us (0.900)
  Pallas kernels: 74.7 us -> 70.3 us
  local copies, waits for them, and re-layouts: 6.82 us -> 3.11 us
    pallas_call x1, Pallas kernels: 74.7 us -> 70.3 us  [step(): pl.pallas_call(functools.partial(step_kernel, layers, m, lo, hi, tokens *...]
    unnamed x10 -> x2, local copies, waits for them, and re-layouts: 6.82 us -> 3.11 us
where the time goes in v3:
time: 74.2 us; the launch traced here: 74.1 us
  Pallas kernels  70.3 us (95%)
  local copies, waits for them, and re-layouts  3.11 us (4%)
    pallas_call x1, Pallas kernels, step(): pl.pallas_call(functools.partial(step_kernel, layers, m, lo, hi, tokens *...  70.3 us
    unnamed x2, local copies, waits for them, and re-layouts  3.11 us

profile of v3, /device:TPU:1, one launch (start us, length us, event | category | flops | bytes accessed | tf_op | source)
XLA Modules:
  0.0 74.1 jit_solution(17298571106529707570)
XLA Ops:
  0.6 70.3 %step.1 = (f32[3,32,1024]{2,1,0:T(8,128)S(1)}, bf16[1024,2560]{1,0:T(8,128)(2,1)S(1)}) custom-call(bf16[2,2,2,3,32,1024]{5,4,3,2,1,0:T(8,128)(2,1)} %bitcast.10, bf16[1024,2560]{1,0:T(8,128)(2,1)} %bitcast.9, bf16[2560,2,1024]{2,1,0:T(2,128)(2,1)} %bitcast.8, f32[1,2560]{1,0:T(1,128)} %enc_bias_hbm.1, bf16[3,32,1024]{2,1,0:T(8,128)(2,1)} %bitcast.11, ...), custom_call_target="tpu_custom_call" | custom-call | tf_op jit(solution)/shard_map/step/pallas_call | solution.py:416
  71.0 0.7 %copy.10 = f32[1,96,1024]{2,1,0:T(8,128)} copy(f32[1,96,1024]{2,1,0:T(8,128)S(1)} %bitcast.7) | data formatting | bytes 786432
  71.7 2.4 %copy.11 = bf16[1,1024,2560]{2,1,0:T(8,128)(2,1)} copy(bf16[1,1024,2560]{2,1,0:T(8,128)(2,1)S(1)} %bitcast.6) | data formatting | bytes 10485760

commit v4 on v3

--- a/solution.py
+++ b/solution.py
@@ -1,4 +1,5 @@
 import functools
+import math
 
 import jax
 import jax.numpy as jnp
@@ -31,22 +32,22 @@
 
 
 SPOTS = {
-    "x": (3, 4, 6, 6),
-    "low": (5, 7, 10, 10),
-    "high": (8, 10, 12, 12),
-    "give_z": (11, 13, 15, 15),
-    "give_x": (15, 21, 23, 18),
-    "down": (28, 23, 29, 24),
+    "x": (2, 4, 5, 6),
+    "low": (5, 6, 9, 9),
+    "high": (9, 10, 11, 12),
+    "give_z": (11, 12, 14, 15),
+    "give_x": (14, 29, 23, 26),
+    "down": (32, 31, 33, 44),
 }
 REST = {
-    "x": ((0, 0, 0, 0), (0, 0, 0, 0), (0, 1, 2, 0)),
-    "low": ((0, 0, 0, 0), (0, 0, 4, 3), (6, 10, 9, 20)),
-    "high": ((0, 0, 0, 0), (0, 5, 7, 11), (18, 26, 25, 38)),
-    "give_z": ((0, 0, 0, 0), (8, 12, 19, 27), (30, 36, 41, 47)),
-    "give_x": ((0, 16, 17, 22), (33, 28, 40, 35), (55, 51, 54, 58)),
-    "down": ((32, 23, 24, 31), (44, 43, 50, 49), (61, 57, 60, 63)),
-    "gradient": ((34, 42), (56, 59), (65, 66)),
-    "weigh": ((46, 52), (62, 64), (67, 68)),
+    "x": ((0, 0, 0, 0), (0, 0, 0, 0), (0, 1, 0, 3)),
+    "low": ((0, 0, 0, 0), (0, 0, 0, 0), (10, 15, 9, 27)),
+    "high": ((0, 0, 0, 0), (0, 2, 4, 8), (22, 25, 24, 34)),
+    "give_z": ((0, 0, 0, 0), (5, 6, 21, 23), (35, 39, 42, 49)),
+    "give_x": ((0, 16, 14, 19), (30, 26, 40, 38), (50, 53, 52, 56)),
+    "down": ((31, 20, 18, 28), (41, 33, 47, 48), (57, 60, 59, 62)),
+    "gradient": ((32, 44), (54, 58), (64, 65)),
+    "weigh": ((45, 51), (61, 63), (66, 67)),
 }
 
 
@@ -172,11 +173,14 @@
     def encode(c, t):
         lhs = acts[c].reshape(block, width)
         pre = jnp.dot(lhs, enc[:, feats(t)], preferred_element_type=jnp.float32)
-        scaled = 4.0 * (pre + enc_bias_ref[:, feats(t)])
-        shrunk = jnp.exp(-jnp.abs(scaled))
-        latent[:, feats(t)] = ((jnp.maximum(scaled, 0.0) + jnp.log1p(shrunk)) * 0.25).astype(jnp.bfloat16)
-        part = 1.0 / (1.0 + shrunk)
-        deriv[c, :, feats(t)] = jnp.where(scaled >= 0.0, part, shrunk * part).astype(jnp.bfloat16)
+        pre = pre + enc_bias_ref[:, feats(t)]
+        shrunk = jnp.exp2(jnp.abs(pre) * (-4.0 * math.log2(math.e)))
+        grown = 1.0 + shrunk
+        part = 1.0 / grown
+        lost = shrunk - (grown - 1.0)
+        soft = jnp.log2(grown) * (0.25 * math.log(2.0)) + lost * (part * 0.25)
+        latent[:, feats(t)] = (jnp.maximum(pre, 0.0) + soft).astype(jnp.bfloat16)
+        deriv[c, :, feats(t)] = jnp.where(pre >= 0.0, part, shrunk * part).astype(jnp.bfloat16)
 
     def decode_later(c, d):
         value = jnp.dot(latent[...], dec[1, :, dots(d)], preferred_element_type=jnp.float32)

time: 74.2 us -> 76.1 us (1.026)
  Pallas kernels: 70.3 us -> 72.2 us
    pallas_call x1, Pallas kernels: 70.3 us -> 72.2 us  [step(): pl.pallas_call(functools.partial(step_kernel, layers, m, lo, hi, tokens *...]
where the time goes in v4:
time: 76.1 us; the launch traced here: 76 us
  Pallas kernels  72.2 us (95%)
  local copies, waits for them, and re-layouts  3.11 us (4%)
    pallas_call x1, Pallas kernels, step(): pl.pallas_call(functools.partial(step_kernel, layers, m, lo, hi, tokens *...  72.2 us
    unnamed x2, local copies, waits for them, and re-layouts  3.11 us

profile of v4, /device:TPU:1, one launch (start us, length us, event | category | flops | bytes accessed | tf_op | source)
XLA Modules:
  0.0 76.0 jit_solution(5195866622558688689)
XLA Ops:
  0.6 72.2 %step.1 = (f32[3,32,1024]{2,1,0:T(8,128)S(1)}, bf16[1024,2560]{1,0:T(8,128)(2,1)S(1)}) custom-call(bf16[2,2,2,3,32,1024]{5,4,3,2,1,0:T(8,128)(2,1)} %bitcast.10, bf16[1024,2560]{1,0:T(8,128)(2,1)} %bitcast.9, bf16[2560,2,1024]{2,1,0:T(2,128)(2,1)} %bitcast.8, f32[1,2560]{1,0:T(1,128)} %enc_bias_hbm.1, bf16[3,32,1024]{2,1,0:T(8,128)(2,1)} %bitcast.11, ...), custom_call_target="tpu_custom_call" | custom-call | tf_op jit(solution)/shard_map/step/pallas_call | solution.py:420
  72.9 0.7 copy.10
  73.6 2.4 %copy.11 = bf16[1,1024,2560]{2,1,0:T(8,128)(2,1)} copy(bf16[1,1024,2560]{2,1,0:T(8,128)(2,1)S(1)} %bitcast.6) | data formatting | bytes 10485760

commit v5 on v4

--- a/solution.py
+++ b/solution.py
@@ -32,22 +32,23 @@
 
 
 SPOTS = {
-    "x": (2, 4, 5, 6),
-    "low": (5, 6, 9, 9),
-    "high": (9, 10, 11, 12),
-    "give_z": (11, 12, 14, 15),
-    "give_x": (14, 29, 23, 26),
-    "down": (32, 31, 33, 44),
+    "x": (3, 4, 6, 6),
+    "low": (5, 7, 9, 9),
+    "high": (8, 10, 12, 12),
+    "give_z": (10, 13, 17, 15),
+    "give_x": (14, 16, 20, 19),
+    "down": (47, 29, 23, 26),
 }
 REST = {
-    "x": ((0, 0, 0, 0), (0, 0, 0, 0), (0, 1, 0, 3)),
-    "low": ((0, 0, 0, 0), (0, 0, 0, 0), (10, 15, 9, 27)),
-    "high": ((0, 0, 0, 0), (0, 2, 4, 8), (22, 25, 24, 34)),
-    "give_z": ((0, 0, 0, 0), (5, 6, 21, 23), (35, 39, 42, 49)),
-    "give_x": ((0, 16, 14, 19), (30, 26, 40, 38), (50, 53, 52, 56)),
-    "down": ((31, 20, 18, 28), (41, 33, 47, 48), (57, 60, 59, 62)),
-    "gradient": ((32, 44), (54, 58), (64, 65)),
-    "weigh": ((45, 51), (61, 63), (66, 67)),
+    "x": ((0, 0, 0, 0), (0, 0, 0, 0), (0, 0, 2, 1)),
+    "low": ((0, 0, 0, 0), (0, 0, 0, 0), (8, 10, 16, 13)),
+    "high": ((0, 0, 0, 0), (0, 5, 9, 14), (19, 22, 31, 28)),
+    "give_z": ((0, 0, 3, 0), (7, 11, 20, 26), (32, 37, 46, 44)),
+    "give_x": ((0, 6, 12, 21), (18, 30, 39, 41), (51, 53, 55, 54)),
+    "down": ((25, 15, 23, 29), (27, 43, 49, 48), (58, 59, 61, 62)),
+    "contribute": ((33, 0), (56, 0), (65, 0)),
+    "gradient": ((34, 42), (57, 60), (66, 67)),
+    "weigh": ((47, 52), (63, 64), (68, 69)),
 }
 
 
@@ -67,6 +68,7 @@
             rest += [(stage, c, h) for c in range(chunks) if c + back > final]
     for spot in inside:
         spot.sort(key=lambda e: -e[0])
+    rest += [("contribute", c, 0) for c in range(chunks)]
     rest += [(stage, c, t) for c in range(chunks) for stage in ("gradient", "weigh") for t in range(tiles)]
     return inside, sorted(rest, key=lambda e: rank(*e))
 
@@ -267,6 +269,9 @@
             for q in range(1, m):
                 down(c, h, q).start()
 
+    def contribute(c, t):
+        own[:, :tile] = contract_width(gath[c].reshape(block, width), dec[0, feats(t), :])
+
     def gradient(c, t):
         if t == 0:
             @pl.when(layer < layers - 1)
@@ -275,7 +280,9 @@
                     for q in range(m):
                         down(c, h, q).wait_recv()
 
-        grad = contract_width(gath[c].reshape(block, width), dec[0, feats(t), :])
+            grad = own[:, :tile]
+        else:
+            grad = contract_width(gath[c].reshape(block, width), dec[0, feats(t), :])
         grad = grad + contract_width(foll[c].reshape(block, width), dec[1, feats(t), :])
         latent[:, feats(t)] = (grad * deriv[c, :, feats(t)].astype(jnp.float32)).astype(jnp.bfloat16)
 
@@ -293,7 +300,7 @@
 
     run = {
         "x": send_x, "low": send_low, "high": send_high, "give_z": send_errors,
-        "give_x": pass_x, "down": pass_down, "gradient": gradient, "weigh": weigh,
+        "give_x": pass_x, "down": pass_down, "contribute": contribute, "gradient": gradient, "weigh": weigh,
     }
     inside, rest = plan(chunks, tiles)
 
@@ -309,8 +316,7 @@
     for copy in every(0):
         copy.start()
     small[0].start()
-    for t in range(tiles):
-        load_enc(t).start()
+    load_enc(0).start()
 
     @pl.when(layer == layers - 1)
     def _():
@@ -330,6 +336,8 @@
     load_enc(0).wait()
     for i in range(slots):
         load_dec(i).start()
+    for t in range(1, tiles):
+        load_enc(t).start()
     for copy in small[1:]:
         copy.start()
     for c in range(1, chunks):
@@ -434,7 +442,7 @@
             pltpu.VMEM((2, features, width), half),
             pltpu.VMEM((chunks, block, features), half),
             pltpu.VMEM((block, features), half),
-            pltpu.VMEM((block, width), full),
+            pltpu.VMEM((block, max(width, tile_of(features))), full),
             pltpu.VMEM((width, features), full),
             pltpu.VMEM((chunks, m, lo, hi, rows, width), half),
             pltpu.VMEM((chunks, m, lo, hi, rows, width), half),

time: 76.1 us -> 73 us (0.959)
  Pallas kernels: 72.2 us -> 69.1 us
    pallas_call x1, Pallas kernels: 72.2 us -> 69.1 us  [step(): pl.pallas_call(functools.partial(step_kernel, layers, m, lo, hi, tokens *...]
where the time goes in v5:
time: 73 us; the launch traced here: 72.9 us
  Pallas kernels  69.1 us (95%)
  local copies, waits for them, and re-layouts  3.11 us (4%)
    pallas_call x1, Pallas kernels, step(): pl.pallas_call(functools.partial(step_kernel, layers, m, lo, hi, tokens *...  69.1 us
    unnamed x2, local copies, waits for them, and re-layouts  3.11 us

profile of v5, /device:TPU:1, one launch (start us, length us, event | category | flops | bytes accessed | tf_op | source)
XLA Modules:
  0.0 72.9 jit_solution(9263985124163675695)
XLA Ops:
  0.6 69.1 %step.1 = (f32[3,32,1024]{2,1,0:T(8,128)S(1)}, bf16[1024,2560]{1,0:T(8,128)(2,1)S(1)}) custom-call(bf16[2,2,2,3,32,1024]{5,4,3,2,1,0:T(8,128)(2,1)} %bitcast.10, bf16[1024,2560]{1,0:T(8,128)(2,1)} %bitcast.9, bf16[2560,2,1024]{2,1,0:T(2,128)(2,1)} %bitcast.8, f32[1,2560]{1,0:T(1,128)} %enc_bias_hbm.1, bf16[3,32,1024]{2,1,0:T(8,128)(2,1)} %bitcast.11, ...), custom_call_target="tpu_custom_call" | custom-call | tf_op jit(solution)/shard_map/step/pallas_call | solution.py:428
  69.8 0.7 %copy.10 = f32[1,96,1024]{2,1,0:T(8,128)} copy(f32[1,96,1024]{2,1,0:T(8,128)S(1)} %bitcast.7) | data formatting | bytes 786432
  70.5 2.4 %copy.11 = bf16[1,1024,2560]{2,1,0:T(8,128)(2,1)} copy(bf16[1,1024,2560]{2,1,0:T(8,128)(2,1)S(1)} %bitcast.6) | data formatting | bytes 10485760

commit v6 on v5

--- a/solution.py
+++ b/solution.py
@@ -32,23 +32,23 @@
 
 
 SPOTS = {
-    "x": (3, 4, 6, 6),
-    "low": (5, 7, 9, 9),
-    "high": (8, 10, 12, 12),
-    "give_z": (10, 13, 17, 15),
-    "give_x": (14, 16, 20, 19),
-    "down": (47, 29, 23, 26),
+    "x": (2, 4, 5, 7),
+    "low": (6, 7, 8, 10),
+    "high": (9, 10, 12, 14),
+    "give_z": (11, 13, 22, 18),
+    "give_x": (19, 26, 35, 29),
+    "down": (48, 31, 65, 54),
 }
 REST = {
-    "x": ((0, 0, 0, 0), (0, 0, 0, 0), (0, 0, 2, 1)),
-    "low": ((0, 0, 0, 0), (0, 0, 0, 0), (8, 10, 16, 13)),
-    "high": ((0, 0, 0, 0), (0, 5, 9, 14), (19, 22, 31, 28)),
-    "give_z": ((0, 0, 3, 0), (7, 11, 20, 26), (32, 37, 46, 44)),
-    "give_x": ((0, 6, 12, 21), (18, 30, 39, 41), (51, 53, 55, 54)),
-    "down": ((25, 15, 23, 29), (27, 43, 49, 48), (58, 59, 61, 62)),
-    "contribute": ((33, 0), (56, 0), (65, 0)),
-    "gradient": ((34, 42), (57, 60), (66, 67)),
-    "weigh": ((47, 52), (63, 64), (68, 69)),
+    "x": ((0, 0, 0, 0), (0, 0, 0, 0), (0, 2, 1, 5)),
+    "low": ((0, 0, 0, 0), (0, 0, 0, 0), (12, 13, 18, 21)),
+    "high": ((0, 0, 0, 0), (0, 3, 11, 14), (22, 26, 30, 42)),
+    "give_z": ((0, 0, 7, 9), (16, 20, 23, 28), (39, 41, 44, 53)),
+    "give_x": ((4, 6, 15, 19), (35, 33, 38, 45), (52, 55, 58, 62)),
+    "down": ((17, 27, 29, 31), (43, 47, 50, 54), (60, 64, 65, 66)),
+    "contribute": ((32, 0), (56, 0), (67, 0)),
+    "gradient": ((36, 40), (59, 63), (70, 71)),
+    "weigh": ((46, 48), (68, 69), (72, 73)),
 }
 
 
@@ -316,7 +316,8 @@
     for copy in every(0):
         copy.start()
     small[0].start()
-    load_enc(0).start()
+    for t in range(tiles):
+        load_enc(t).start()
 
     @pl.when(layer == layers - 1)
     def _():
@@ -336,8 +337,6 @@
     load_enc(0).wait()
     for i in range(slots):
         load_dec(i).start()
-    for t in range(1, tiles):
-        load_enc(t).start()
     for copy in small[1:]:
         copy.start()
     for c in range(1, chunks):

time: 73 us -> 70.9 us (0.971)
  Pallas kernels: 69.1 us -> 67 us
    pallas_call x1, Pallas kernels: 69.1 us -> 67 us  [step(): pl.pallas_call(functools.partial(step_kernel, layers, m, lo, hi, tokens *...]
where the time goes in v6:
time: 70.9 us; the launch traced here: 70.8 us
  Pallas kernels  67 us (94%)
  local copies, waits for them, and re-layouts  3.11 us (4%)
    pallas_call x1, Pallas kernels, step(): pl.pallas_call(functools.partial(step_kernel, layers, m, lo, hi, tokens *...  67 us
    unnamed x2, local copies, waits for them, and re-layouts  3.11 us

profile of v6, /device:TPU:1, one launch (start us, length us, event | category | flops | bytes accessed | tf_op | source)
XLA Modules:
  0.0 70.8 jit_solution(9644104279125336268)
XLA Ops:
  0.6 67.0 %step.1 = (f32[3,32,1024]{2,1,0:T(8,128)S(1)}, bf16[1024,2560]{1,0:T(8,128)(2,1)S(1)}) custom-call(bf16[2,2,2,3,32,1024]{5,4,3,2,1,0:T(8,128)(2,1)} %bitcast.10, bf16[1024,2560]{1,0:T(8,128)(2,1)} %bitcast.9, bf16[2560,2,1024]{2,1,0:T(2,128)(2,1)} %bitcast.8, f32[1,2560]{1,0:T(1,128)} %enc_bias_hbm.1, bf16[3,32,1024]{2,1,0:T(8,128)(2,1)} %bitcast.11, ...), custom_call_target="tpu_custom_call" | custom-call | tf_op jit(solution)/shard_map/step/pallas_call | solution.py:427
  67.7 0.7 %copy.10 = f32[1,96,1024]{2,1,0:T(8,128)} copy(f32[1,96,1024]{2,1,0:T(8,128)S(1)} %bitcast.7) | data formatting | bytes 786432
  68.4 2.4 %copy.11 = bf16[1,1024,2560]{2,1,0:T(8,128)(2,1)} copy(bf16[1,1024,2560]{2,1,0:T(8,128)(2,1)S(1)} %bitcast.6) | data formatting | bytes 10485760
